TPU v7x, 32 devices: a whole 2x2x4 slice. The times are simulated.
32 devices in a mesh: parts: 2 (over y), sub: 4 (over z), row: 2 (over x), col: 2 (over core).
Axes of the slice: x: 2, y: 2, z: 4, core: 2. Of those that a mesh axis runs over, the one named last changes fastest.
Arguments:
- loads: float32 [8, 32, 1024], P(('parts', 'sub'), 'col'), parts along dimension 0, may hold values from -6 to 6
- weights: float32 [8, 1024], P(('parts', 'sub')), parts along dimension 0, may hold values from 0.25 to 4
- dual_ops: bfloat16 [8, 2048, 2048], P(('parts', 'sub'), 'row'), parts along dimension 0, as said below
- corner_maps: bfloat16 [8, 24, 2048], P(('parts', 'sub'), None, 'row'), parts along dimension 0, may hold values from -0.25 to 0.25
- coarse_inverse: float32 [96, 48], P('parts'), parts along dimension 0, as said below
- corner_ids: int32 [8, 24], P('parts'), parts along dimension 0, may hold values from 0 to 47, as said below
- iface_sizes: int32 [8], P('parts'), parts along dimension 0, may hold values from 512 to 1024, as said below
- left_partner: int32 [8, 1024], P(('parts', 'sub')), parts along dimension 0, may hold values from 0 to 1023, as said below
- right_partner: int32 [8, 1024], P(('parts', 'sub')), parts along dimension 0, may hold values from 0 to 1023, as said below
Outputs:
- solution: float32 [8, 32, 1024], P(('parts', 'sub'), 'col'), parts along dimension 0
- residual: float32 [8, 32, 1024], P(('parts', 'sub'), 'col'), parts along dimension 0
There are 2 independent parts, one for each index of `parts`. A program takes and returns all parts, laid end to end along the dimension named above; each array names one. Nothing has to cross between parts.
Inputs may be any that keep to these rules, and one draw needn't show every extreme that they name: Global indices 24/2 * s to 24/2 * s + 24/2 - 1 are the corners of the interface between s and s+1; the first half of subdomain s's corner_ids is a permutation of those of interface s-1, the second half a permutation of those of interface s. `left_partner`: each row s is a permutation that maps the slots below iface_sizes[s-1] onto slots below it. `right_partner`: each row s is a permutation that maps the slots below iface_sizes[s] onto slots below it, and is the inverse of left_partner[s+1]. `dual_ops`: symmetric positive definite. `coarse_inverse`: symmetric positive definite. For each s < 2, one of iface_sizes[s] and iface_sizes[s + 2] is 896 or more and the other 640 or less.
All inputs are finite; a program needn't handle non-finite values.
Results may differ from a plain program's by a relative error of at most 0.015.
Values may be sent and summed in bfloat16 or wider, within the bound.
No kernel may reach another device: no remote copies, remote signals or barrier semaphores. Data moves between devices by JAX's collectives and lax.ppermute only.
A program may use at most 64 MiB of HBM per device.

v0:
```python
import jax
import jax.numpy as jnp
from jax import lax
from jax.sharding import PartitionSpec as P

TILE = 128
ITERS = 2


def shifted(value, axis, steps):
    count = lax.axis_size(axis)
    pairs = [(source, (source + steps) % count) for source in range(count)]
    return lax.ppermute(value, axis, pairs)


def inner(first, second, half):
    return jnp.sum(first[:, :half] * second[:, :half], axis=1)


def paired_totals(residual, precond, image, half):
    return lax.psum((inner(residual, precond, half), inner(precond, image, half)), "sub")


def tile_products(vector, rows_op, first_tile, last_tile, output):

    def one_tile(tile_at, acc):
        piece = lax.dynamic_slice_in_dim(rows_op, tile_at * TILE, TILE, 0)
        product = lax.dot_general(
            vector, piece, (((1,), (1,)), ((), ())), preferred_element_type=jnp.float32
        )
        return lax.dynamic_update_slice_in_dim(acc, product, tile_at * TILE, 1)

    return lax.fori_loop(first_tile, last_tile, one_tile, output)


def live_tiles(size_before, size_after, block_start, block, half):
    left_live = jnp.clip(size_before - block_start, 0, block)
    right_live = jnp.clip(size_after - (block_start - half), 0, block)
    live_cols = jnp.where(block_start < half, left_live, right_live)
    return (live_cols + TILE - 1) // TILE


def per_device(
    loads,
    weights,
    dual_ops,
    corner_maps,
    coarse_inverse,
    corner_ids,
    iface_sizes,
    left_partner,
    right_partner,
):
    half = loads.shape[2]
    block = dual_ops.shape[1]
    width = coarse_inverse.shape[0]
    subdomain = lax.axis_index("sub")
    count = lax.axis_size("sub")
    row_index = lax.axis_index("row")
    left_map = left_partner[0]
    right_map = right_partner[0]
    slots = jnp.arange(half, dtype=jnp.int32)
    size_before = iface_sizes[(subdomain + count - 1) % count]
    size_after = iface_sizes[subdomain]
    live_left = (slots < size_before).astype(jnp.float32)
    live_right = (right_map < size_after).astype(jnp.float32)
    columns = jnp.arange(width, dtype=jnp.int32)
    own_hot = (corner_ids[subdomain][:, None] == columns[None, :]).astype(jnp.float32)
    operator = dual_ops[0]
    coupling = corner_maps[0]
    block_start = row_index * block
    own_tiles = live_tiles(size_before, size_after, block_start, block, half)

    def apply_operator(vec):
        halfway = vec.astype(jnp.bfloat16)
        empty = jnp.zeros((halfway.shape[0], block), jnp.float32)
        local = tile_products(halfway, operator, jnp.int32(0), own_tiles, empty)
        own_slots = lax.dynamic_slice_in_dim(halfway, row_index * block, block, 1)
        corner = lax.dot_general(
            own_slots, coupling, (((1,), (1,)), ((), ())), preferred_element_type=jnp.float32
        )
        scattered = jnp.dot(corner, own_hot, precision=lax.Precision.HIGHEST)
        coarse = lax.psum(scattered, ("sub", "row"))
        solved = jnp.dot(coarse, coarse_inverse, precision=lax.Precision.HIGHEST)
        back = lax.dot_general(
            solved, own_hot, (((1,), (1,)), ((), ())), precision=lax.Precision.HIGHEST
        ).astype(jnp.bfloat16)
        united = local + jnp.dot(back, coupling, preferred_element_type=jnp.float32)
        whole = lax.all_gather(united.astype(jnp.bfloat16), "row", axis=1, tiled=True).astype(
            united.dtype
        )
        lower = whole[:, :half]
        upper = whole[:, half:]
        arrived_left = shifted(upper.astype(jnp.bfloat16), "sub", 1).astype(upper.dtype)
        arrived_right = shifted(lower.astype(jnp.bfloat16), "sub", -1).astype(lower.dtype)
        result_left = (lower + jnp.take(arrived_left, left_map, axis=1)) * live_left
        result_right = (upper + jnp.take(arrived_right, right_map, axis=1)) * live_right
        return jnp.concatenate([result_left, result_right], axis=1)

    received = (
        shifted(loads[0].astype(jnp.bfloat16), "sub", -1).astype(jnp.float32),
        shifted(weights.astype(jnp.bfloat16), "sub", -1).astype(weights.dtype),
    )
    right_load = jnp.take(received[0], right_map, axis=1) * live_right
    right_weight = jnp.take(received[1], right_map, axis=1)
    residual = jnp.concatenate([loads[0] * live_left, right_load], axis=1)
    scaling = jnp.concatenate([weights, right_weight], axis=1)
    solution = jnp.zeros_like(residual)
    precond = scaling * residual
    image = apply_operator(precond)
    gamma, delta = paired_totals(residual, precond, image, half)
    alpha = gamma / delta
    direction = precond
    along = image
    for step in range(ITERS):
        solution = solution + alpha[:, None] * direction
        residual = residual - alpha[:, None] * along
        if step + 1 < ITERS:
            precond = scaling * residual
            image = apply_operator(precond)
            gamma_next, delta = paired_totals(residual, precond, image, half)
            ratio = gamma_next / gamma
            alpha = gamma_next / (delta - ratio * gamma_next / alpha)
            direction = precond + ratio[:, None] * direction
            along = image + ratio[:, None] * along
            gamma = gamma_next
    return (solution[:, :half][None], residual[:, :half][None])


def solution(mesh):
    placed = (
        P(("parts", "sub"), "col", None),
        P(("parts", "sub"), None),
        P(("parts", "sub"), "row", None),
        P(("parts", "sub"), None, "row"),
        P("parts", None),
        P("parts", None),
        P("parts"),
        P(("parts", "sub"), None),
        P(("parts", "sub"), None),
    )
    return jax.shard_map(
        per_device,
        mesh=mesh,
        in_specs=placed,
        out_specs=(P(("parts", "sub"), "col", None), P(("parts", "sub"), "col", None)),
        check_vma=False,
    )
```

profile of v0, /device:TPU:0, one launch (start us, length us, event | category | flops | bytes accessed | tf_op | source)
XLA Modules:
  0.0 136.2 jit_solution(17909804324471528583)
XLA Ops:
  0.7 0.9 bitcast_convert_fusion
  1.5 5.1 %collective-permute-start.1 = (bf16[16,1024]{1,0:T(8,128)(2,1)S(1)}, bf16[16,1024]{1,0:T(8,128)(2,1)S(1)}, u32[]{:S(2)}, u32[]{:S(2)}) collective-permute-start(bf16[16,1024]{1,0:T(8,128)(2,1)S(1)} %bitcast_convert_fusion), channel_id=1, source_target_pairs={{0,12},{4,0},{8,4},{12,8},{1,13},{5,1},{9,5},{13,9},{2,14},{6,2},{... | collective-permute-start | bytes 98312 | tf_op jit(solution)/shard_map/ppermute | solution.py:13
  6.6 0.7 convert_element_type.71
  7.3 0.4 collective-permute-start
  7.8 0.7 compare_select_fusion
  8.4 0.7 fusion.36
  9.1 1.3 fusion.49
  10.5 1.3 fusion.35
  11.8 1.3 compare_convert_fusion
  13.1 0.8 bitcast_multiply_fusion.1
  14.0 0.7 fusion.40
  14.7 0.7 fusion.37
  16.7 4.5 %gather_fusion = f32[1024]{0:T(1024)S(1)} fusion(f32[1024]{0:T(1024)S(1)} %bitcast.80, s32[1024]{0:T(1024)S(1)} %broadcast_clamp_fusion), kind=kCustom, calls=%fused_computation.5 | custom fusion | bytes 12288 | tf_op jit(solution)/shard_map/jit(_take)/gather | solution.py:105
  21.4 0.1 copy.21
  21.5 2.8 %gather_fusion.1 = f32[1024,16]{1,0:T(8,128)S(1)} fusion(f32[16,1024]{0,1:T(8,128)S(1)} %copy.21, s32[1024]{0:T(1024)S(1)} %fusion.36), kind=kCustom, calls=%fused_computation.clone | custom fusion | bytes 135168 | tf_op jit(solution)/shard_map/jit(_take)/gather | solution.py:104
  24.3 0.2 copy.22
  24.5 10.4 %while.20 = (s32[]{:T(128)}, f32[16,1024]{1,0:T(8,128)S(1)}, s32[]{:T(128)}, bf16[1024,2048]{1,0:T(8,128)(2,1)}, bf16[16,2048]{1,0:T(8,128)(2,1)S(1)}, /*index=5*/s32[]{:T(128)}, s32[]{:T(128)}, s32[]{:T(128)}, s32[]{:T(128)}) while((s32[]{:T(128)}, f32[16,1024]{1,0:T(8,128)S(1)}, s32[]{:T(128)}, bf16[1024,2048]{1,0:T(8,128)(2,1)}, ...), condition=%wide.region_3.5_spmd, body=%wide.region_2.4_spmd.sunk | while | flops 8388614 | bytes 599179 | solution.py:33
  24.6 1.3 fusion.72
  25.9 1.3 fusion.72
  27.1 1.3 fusion.72
  28.4 1.3 fusion.72
  29.7 1.3 fusion.72
  31.0 1.3 fusion.72
  32.3 1.3 fusion.72
  33.6 1.3 fusion.72
  34.9 0.1 fusion.25
  35.1 0.2 fusion.30
  35.3 18.9 %psum.43 = f32[16,48]{1,0:T(8,128)S(1)} all-reduce(f32[16,48]{1,0:T(8,128)S(1)} %fusion.30), channel_id=1, replica_groups=mesh['parts'=2,'sub'=4,'row'=2,'col'=2] {'sub','row'}, use_global_device_ids=true, to_apply=%region_4.6 | all-reduce | flops 768 | bytes 6144 | tf_op jit(solution)/shard_map/psum | solution.py:83
  54.3 0.2 convolution_convert_fusion.1
  54.5 0.1 fusion.6
  54.6 4.6 %all_gather.6 = bf16[16,2048]{1,0:T(8,128)(2,1)S(1)} all-gather(bf16[16,1024]{1,0:T(8,128)(2,1)S(1)} %fusion.6), channel_id=1, replica_groups=mesh['parts'=2,'sub'=4,'row'=2,'col'=2] {'row'}, dimensions={1}, use_global_device_ids=true | all-gather | bytes 98304 | tf_op jit(solution)/shard_map/all_gather | solution.py:89
  59.2 3.8 %collective-permute-start.3 = (bf16[16,1024]{1,0:T(8,128)(2,1)S(1)}, bf16[16,1024]{1,0:T(8,128)(2,1)S(1)}, u32[]{:S(2)}, u32[]{:S(2)}) collective-permute-start(bf16[16,1024]{1,0:T(8,128)(2,1)S(1)} %get-tuple-element.103), channel_id=1, source_target_pairs={{0,12},{4,0},{8,4},{12,8},{1,13},{5,1},{9,5},{13,9},{2,14},{6,2},{... | collective-permute-start | bytes 98312 | tf_op jit(solution)/shard_map/ppermute | solution.py:13
  63.1 1.9 %collective-permute-done.2 = bf16[16,1024]{1,0:T(8,128)(2,1)S(1)} collective-permute-done((bf16[16,1024]{1,0:T(8,128)(2,1)S(1)}, bf16[16,1024]{1,0:T(8,128)(2,1)S(1)}, u32[]{:S(2)}, u32[]{:S(2)}) %collective-permute-start.2) | collective-permute-done | bytes 32800 | tf_op jit(solution)/shard_map/ppermute | solution.py:13
  65.1 2.8 %gather_fusion.2 = f32[1024,16]{1,0:T(8,128)S(1)} fusion(f32[16,1024]{0,1:T(8,128)S(1)} %copy.23, s32[1024]{0:T(1024)S(1)} %fusion.37), kind=kCustom, calls=%fused_computation.1.clone | custom fusion | bytes 135168 | tf_op jit(solution)/shard_map/jit(_take)/gather | solution.py:96
  67.9 0.2 copy.24
  68.1 0.1 copy.25
  68.2 2.8 %gather_fusion.3 = f32[1024,16]{1,0:T(8,128)S(1)} fusion(f32[16,1024]{0,1:T(8,128)S(1)} %copy.25, s32[1024]{0:T(1024)S(1)} %fusion.36), kind=kCustom, calls=%fused_computation.2.clone | custom fusion | bytes 135168 | tf_op jit(solution)/shard_map/jit(_take)/gather | solution.py:97
  71.0 0.2 copy.26
  71.2 0.1 multiply_reduce_fusion.2
  71.3 9.1 %all-reduce.1 = (f32[16]{0:T(128)S(1)}, f32[16]{0:T(128)S(1)}) all-reduce(f32[16]{0:T(128)S(1)} %get-tuple-element.64, f32[16]{0:T(128)S(1)} %get-tuple-element.63), channel_id=1, replica_groups=mesh['parts'=2,'sub'=4,'row'=2,'col'=2] {'sub'}, use_global_device_ids=true, to_apply=%region_1.3 | all-reduce | flops 32 | bytes 256 | tf_op jit(solution)/shard_map/psum | solution.py:21
  80.6 10.3 %while.21 = (s32[]{:T(128)}, f32[16,1024]{1,0:T(8,128)S(1)}, s32[]{:T(128)}, bf16[1024,2048]{1,0:T(8,128)(2,1)}, bf16[16,2048]{1,0:T(8,128)(2,1)S(1)}, /*index=5*/s32[]{:T(128)}, s32[]{:T(128)}, s32[]{:T(128)}, s32[]{:T(128)}) while((s32[]{:T(128)}, f32[16,1024]{1,0:T(8,128)S(1)}, s32[]{:T(128)}, bf16[1024,2048]{1,0:T(8,128)(2,1)}, ...), condition=%wide.region_10.12_spmd, body=%wide.region_9.11_spmd.sunk | while | flops 8388614 | bytes 599179 | solution.py:33
  80.6 1.3 fusion.75
  81.9 1.3 fusion.75
  83.2 1.3 fusion.75
  84.5 1.3 fusion.75
  85.8 1.3 fusion.75
  87.1 1.3 fusion.75
  88.4 1.3 fusion.75
  89.7 1.3 fusion.75
  91.0 0.2 fusion.29
  91.2 18.7 %psum.46 = f32[16,48]{1,0:T(8,128)S(1)} all-reduce(f32[16,48]{1,0:T(8,128)S(1)} %fusion.29), channel_id=1, replica_groups=mesh['parts'=2,'sub'=4,'row'=2,'col'=2] {'sub','row'}, use_global_device_ids=true, to_apply=%region_11.13 | all-reduce | flops 768 | bytes 6144 | tf_op jit(solution)/shard_map/psum | solution.py:83
  110.0 0.2 convolution_convert_fusion
  110.2 0.1 fusion.7
  110.3 4.6 %all_gather.7 = bf16[16,2048]{1,0:T(8,128)(2,1)S(1)} all-gather(bf16[16,1024]{1,0:T(8,128)(2,1)S(1)} %fusion.7), channel_id=1, replica_groups=mesh['parts'=2,'sub'=4,'row'=2,'col'=2] {'row'}, dimensions={1}, use_global_device_ids=true | all-gather | bytes 98304 | tf_op jit(solution)/shard_map/all_gather | solution.py:89
  114.9 2.0 %collective-permute-start.4 = (bf16[16,1024]{1,0:T(8,128)(2,1)S(1)}, bf16[16,1024]{1,0:T(8,128)(2,1)S(1)}, u32[]{:S(2)}, u32[]{:S(2)}) collective-permute-start(bf16[16,1024]{1,0:T(8,128)(2,1)S(1)} %get-tuple-element.101), channel_id=1, source_target_pairs={{0,4},{4,8},{8,12},{12,0},{1,5},{5,9},{9,13},{13,1},{2,6},{6,10},{... | collective-permute-start | bytes 98312 | tf_op jit(solution)/shard_map/ppermute | solution.py:13
  117.0 1.9 %collective-permute-done.5 = bf16[16,1024]{1,0:T(8,128)(2,1)S(1)} collective-permute-done((bf16[16,1024]{1,0:T(8,128)(2,1)S(1)}, bf16[16,1024]{1,0:T(8,128)(2,1)S(1)}, u32[]{:S(2)}, u32[]{:S(2)}) %collective-permute-start.5) | collective-permute-done | bytes 32800 | tf_op jit(solution)/shard_map/ppermute | solution.py:13
  119.0 2.8 %gather_fusion.5 = f32[1024,16]{1,0:T(8,128)S(1)} fusion(f32[16,1024]{0,1:T(8,128)S(1)} %copy.29, s32[1024]{0:T(1024)S(1)} %fusion.36), kind=kCustom, calls=%fused_computation.4.clone | custom fusion | bytes 135168 | tf_op jit(solution)/shard_map/jit(_take)/gather | solution.py:97
  121.8 0.2 copy.30
  122.0 0.1 copy.27
  122.1 2.8 %gather_fusion.4 = f32[1024,16]{1,0:T(8,128)S(1)} fusion(f32[16,1024]{0,1:T(8,128)S(1)} %copy.27, s32[1024]{0:T(1024)S(1)} %fusion.37), kind=kCustom, calls=%fused_computation.3.clone | custom fusion | bytes 135168 | tf_op jit(solution)/shard_map/jit(_take)/gather | solution.py:96
  124.9 0.2 copy.28
  125.1 0.1 multiply_reduce_fusion
  125.3 10.2 %all-reduce = (f32[16]{0:T(128)S(1)}, f32[16]{0:T(128)S(1)}) all-reduce(f32[16]{0:T(128)S(1)} %get-tuple-element.62, f32[16]{0:T(128)S(1)} %get-tuple-element.61), channel_id=1, replica_groups=mesh['parts'=2,'sub'=4,'row'=2,'col'=2] {'sub'}, use_global_device_ids=true, to_apply=%region_8.10 | all-reduce | flops 32 | bytes 256 | tf_op jit(solution)/shard_map/psum | solution.py:21
  135.4 0.7 fusion.16
  (39 shorter events, 1.0 us)
Async XLA Ops:
  0.6 34.3 %copy-start = (bf16[1,24,1024]{2,1,0:T(8,128)(2,1)S(1)}, bf16[1,24,1024]{2,1,0:T(8,128)(2,1)}, u32[]{:S(2)}) copy-start(bf16[1,24,1024]{2,1,0:T(8,128)(2,1)} %param.18) | copy-start | bytes 147460
  0.6 20.7 %copy-start.5 = (f32[1,1024]{1,0:T(1,128)S(1)}, f32[1,1024]{1,0:T(1,128)}, u32[]{:S(2)}) copy-start(f32[1,1024]{1,0:T(1,128)} %param.16) | copy-start | bytes 12292
  0.7 20.6 %copy-start.2 = (s32[1,1024]{1,0:T(1,128)S(1)}, s32[1,1024]{1,0:T(1,128)}, u32[]{:S(2)}) copy-start(s32[1,1024]{1,0:T(1,128)} %param.23) | copy-start | bytes 12292
  1.5 19.8 %collective-permute-start.1 = (bf16[16,1024]{1,0:T(8,128)(2,1)S(1)}, bf16[16,1024]{1,0:T(8,128)(2,1)S(1)}, u32[]{:S(2)}, u32[]{:S(2)}) collective-permute-start(bf16[16,1024]{1,0:T(8,128)(2,1)S(1)} %bitcast_convert_fusion), channel_id=1, source_target_pairs={{0,12},{4,0},{8,4},{12,8},{1,13},{5,1},{9,5},{13,9},{2,14},{6,2},{... | collective-permute-start | bytes 98312 | tf_op jit(solution)/shard_map/ppermute | solution.py:13
  7.3 9.4 %collective-permute-start = (bf16[1,1024]{1,0:T(2,128)(2,1)S(1)}, bf16[1,1024]{1,0:T(2,128)(2,1)S(1)}, u32[]{:S(2)}, u32[]{:S(2)}) collective-permute-start(bf16[1,1024]{1,0:T(2,128)(2,1)S(1)} %convert_element_type.71), channel_id=1, source_target_pairs={{0,12},{4,0},{8,4},{12,8},{1,13},{5,1},{9,5},{13,9},{2,14},{6,2},{... | collective-permute-start | bytes 6152 | tf_op jit(solution)/shard_map/ppermute | solution.py:13
  16.7 37.4 %copy-start.3 = (f32[48,48]{1,0:T(8,128)S(1)}, f32[48,48]{1,0:T(8,128)}, u32[]{:S(2)}) copy-start(f32[48,48]{1,0:T(8,128)} %param.19) | copy-start | bytes 27652
  16.7 46.3 %copy-start.4 = (s32[1,1024]{1,0:T(1,128)S(1)}, s32[1,1024]{1,0:T(1,128)}, u32[]{:S(2)}) copy-start(s32[1,1024]{1,0:T(1,128)} %param.22) | copy-start | bytes 12292
  24.5 46.7 %copy-start.1 = (f32[1,16,1024]{2,1,0:T(8,128)S(1)}, f32[1,16,1024]{2,1,0:T(8,128)}, u32[]{:S(2)}) copy-start(f32[1,16,1024]{2,1,0:T(8,128)} %param.15) | copy-start | bytes 196612
  59.2 5.7 %collective-permute-start.2 = (bf16[16,1024]{1,0:T(8,128)(2,1)S(1)}, bf16[16,1024]{1,0:T(8,128)(2,1)S(1)}, u32[]{:S(2)}, u32[]{:S(2)}) collective-permute-start(bf16[16,1024]{1,0:T(8,128)(2,1)S(1)} %get-tuple-element.102), channel_id=1, source_target_pairs={{0,4},{4,8},{8,12},{12,0},{1,5},{5,9},{9,13},{13,1},{2,6},{6,10},{... | collective-permute-start | bytes 98312 | tf_op jit(solution)/shard_map/ppermute | solution.py:13
  59.2 8.8 %collective-permute-start.3 = (bf16[16,1024]{1,0:T(8,128)(2,1)S(1)}, bf16[16,1024]{1,0:T(8,128)(2,1)S(1)}, u32[]{:S(2)}, u32[]{:S(2)}) collective-permute-start(bf16[16,1024]{1,0:T(8,128)(2,1)S(1)} %get-tuple-element.103), channel_id=1, source_target_pairs={{0,12},{4,0},{8,4},{12,8},{1,13},{5,1},{9,5},{13,9},{2,14},{6,2},{... | collective-permute-start | bytes 98312 | tf_op jit(solution)/shard_map/ppermute | solution.py:13
  114.9 3.9 %collective-permute-start.5 = (bf16[16,1024]{1,0:T(8,128)(2,1)S(1)}, bf16[16,1024]{1,0:T(8,128)(2,1)S(1)}, u32[]{:S(2)}, u32[]{:S(2)}) collective-permute-start(bf16[16,1024]{1,0:T(8,128)(2,1)S(1)} %get-tuple-element.100), channel_id=1, source_target_pairs={{0,12},{4,0},{8,4},{12,8},{1,13},{5,1},{9,5},{13,9},{2,14},{6,2},{... | collective-permute-start | bytes 98312 | tf_op jit(solution)/shard_map/ppermute | solution.py:13
  114.9 7.0 %collective-permute-start.4 = (bf16[16,1024]{1,0:T(8,128)(2,1)S(1)}, bf16[16,1024]{1,0:T(8,128)(2,1)S(1)}, u32[]{:S(2)}, u32[]{:S(2)}) collective-permute-start(bf16[16,1024]{1,0:T(8,128)(2,1)S(1)} %get-tuple-element.101), channel_id=1, source_target_pairs={{0,4},{4,8},{8,12},{12,0},{1,5},{5,9},{9,13},{13,1},{2,6},{6,10},{... | collective-permute-start | bytes 98312 | tf_op jit(solution)/shard_map/ppermute | solution.py:13
where the time goes:
time: 137 us; the launch traced here: 136 us
  blocking collectives  65.9 us (48%)
  matrix products  22.3 us (16%)
  local copies, waits for them, and re-layouts  22.1 us (16%)
  starting transfers between devices  11.4 us (8%)
  other arithmetic  8.41 us (6%)
  waiting for transfers between devices  3.74 us (3%)
  between operations  2.25 us (2%)
    psum x2, blocking collectives, apply_operator(): coarse = lax.psum(scattered, ('sub', 'row'))  37.5 us
    dot_general x16, matrix products, one_tile(): lax.dot_general(vector, piece, (((1,), (1,)), ((), ())), preferred_elemen...  20.7 us
    psum x2, blocking collectives, paired_totals(): lax.psum((inner(residual, precond, half), inner(precond, image, half)), '...  19.2 us
    ppermute x6, starting transfers between devices, shifted(): return lax.ppermute(value, axis, pairs)  11.4 us
    all_gather x2, blocking collectives, apply_operator(): lax.all_gather(united.astype(jnp.bfloat16), 'row', axis=1, tiled=True)  9.15 us
    gather x4, local copies, waits for them, and re-layouts, apply_operator(): jnp.take(arrived_right, right_map, axis=1)  5.95 us
    gather x4, local copies, waits for them, and re-layouts, apply_operator(): result_left = (lower + jnp.take(arrived_left, left_map, axis=1)) * live_left  5.95 us
    gather x1, local copies, waits for them, and re-layouts, per_device(): right_weight = jnp.take(received[1], right_map, axis=1)  4.53 us
  transfers between devices with their start and end apart: 6, of which 2 were waited for; matrix products, arithmetic and copies ran while one was open for 14% of the time, Pallas kernels for 0%

commit v1 on v0

--- a/solution.py
+++ b/solution.py
@@ -86,7 +86,7 @@
             solved, own_hot, (((1,), (1,)), ((), ())), precision=lax.Precision.HIGHEST
         ).astype(jnp.bfloat16)
         united = local + jnp.dot(back, coupling, preferred_element_type=jnp.float32)
-        whole = lax.all_gather(united.astype(jnp.bfloat16), "row", axis=1, tiled=True).astype(
+        whole = jnp.concatenate(lax.all_gather(united.astype(jnp.bfloat16), "row"), axis=1).astype(
             united.dtype
         )
         lower = whole[:, :half]

time: 137 us -> 174 us (1.27)
  local copies, waits for them, and re-layouts: 22.1 us -> 36.8 us
  other arithmetic: 8.41 us -> 21.7 us
  waiting for transfers between devices: 3.74 us -> 12.6 us
    ppermute x6, waiting for transfers between devices: 3.74 us -> 12.6 us  [shifted(): return lax.ppermute(value, axis, pairs)]
    reduce_sum x2, other arithmetic: 0.29 us -> 5.71 us  [inner(): return jnp.sum(first[:, :half] * second[:, :half], axis=1)]
    unnamed x12 -> x16, local copies, waits for them, and re-layouts: 0.04 us -> 3.9 us
    convert_element_type x2, other arithmetic: 0.12 us -> 3.83 us  [apply_operator(): halfway = vec.astype(jnp.bfloat16)]
    convert_element_type x2 -> x7, other arithmetic: 0.02 us -> 3.7 us  [the longest x2 1.82 us: apply_operator(): shifted(upper.astype(jnp.bfloat16), 'sub', 1).astype(upper.dtype)]
    gather x4 -> x2, local copies, waits for them, and re-layouts: 5.95 us -> 9.09 us  [apply_operator(): result_left = (lower + jnp.take(arrived_left, left_map, axis=1)) * live_left]
    gather x4 -> x2, local copies, waits for them, and re-layouts: 5.95 us -> 9.08 us  [apply_operator(): jnp.take(arrived_right, right_map, axis=1)]
    mul x0 -> x3, local copies, waits for them, and re-layouts: none -> 2.73 us  [the longest x1 1.36 us: per_device(): residual = residual - alpha[:, None] * along]
where the time goes in v1:
time: 174 us; the launch traced here: 173 us
  blocking collectives  65.4 us (38%)
  local copies, waits for them, and re-layouts  36.8 us (21%)
  matrix products  22.5 us (13%)
  other arithmetic  21.7 us (12%)
  waiting for transfers between devices  12.6 us (7%)
  starting transfers between devices  11.4 us (7%)
  between operations  2.25 us (1%)
    psum x2, blocking collectives, apply_operator(): coarse = lax.psum(scattered, ('sub', 'row'))  36.8 us
    dot_general x16, matrix products, one_tile(): lax.dot_general(vector, piece, (((1,), (1,)), ((), ())), preferred_elemen...  20.7 us
    psum x2, blocking collectives, paired_totals(): lax.psum((inner(residual, precond, half), inner(precond, image, half)), '...  19.5 us
    ppermute x6, waiting for transfers between devices, shifted(): return lax.ppermute(value, axis, pairs)  12.6 us
    ppermute x6, starting transfers between devices, shifted(): return lax.ppermute(value, axis, pairs)  11.4 us
    all_gather x2, blocking collectives, apply_operator(): lax.all_gather(united.astype(jnp.bfloat16), 'row')  9.15 us
    gather x2, local copies, waits for them, and re-layouts, apply_operator(): result_left = (lower + jnp.take(arrived_left, left_map, axis=1)) * live_left  9.09 us
    gather x2, local copies, waits for them, and re-layouts, apply_operator(): jnp.take(arrived_right, right_map, axis=1)  9.08 us
  transfers between devices with their start and end apart: 6, of which 2 were waited for; matrix products, arithmetic and copies ran while one was open for 14% of the time, Pallas kernels for 0%

profile of v1, /device:TPU:0, one launch (start us, length us, event | category | flops | bytes accessed | tf_op | source)
XLA Modules:
  0.0 172.7 jit_solution(17816688243890508609)
XLA Ops:
  0.7 0.7 convert_element_type.83
  1.4 5.1 %collective-permute-start = (bf16[1,1024]{1,0:T(2,128)(2,1)S(1)}, bf16[1,1024]{1,0:T(2,128)(2,1)S(1)}, u32[]{:S(2)}, u32[]{:S(2)}) collective-permute-start(bf16[1,1024]{1,0:T(2,128)(2,1)S(1)} %convert_element_type.83), channel_id=1, source_target_pairs={{0,12},{4,0},{8,4},{12,8},{1,13},{5,1},{9,5},{13,9},{2,14},{6,2},{... | collective-permute-start | bytes 6152 | tf_op jit(solution)/shard_map/ppermute | solution.py:13
  6.5 1.0 copy.45
  7.6 0.5 collective-permute-start.1
  8.1 0.7 compare_select_fusion
  8.8 0.7 fusion.39
  9.4 1.3 fusion.48
  10.8 1.3 compare_convert_fusion
  12.1 0.7 fusion.35
  12.8 0.7 fusion.36
  13.5 1.3 fusion.34
  16.4 4.5 %gather_fusion = f32[1024]{0:T(1024)S(1)} fusion(f32[1024]{0:T(1024)S(1)} %bitcast.90, s32[1024]{0:T(1024)S(1)} %broadcast_clamp_fusion), kind=kCustom, calls=%fused_computation.5 | custom fusion | bytes 12288 | tf_op jit(solution)/shard_map/jit(_take)/gather | solution.py:105
  21.0 2.8 %gather_fusion.1 = f32[1024,16]{1,0:T(8,128)S(1)} fusion(f32[16,1024]{0,1:T(8,128)S(1)} %convert_element_type.86, s32[1024]{0:T(1024)S(1)} %fusion.35), kind=kCustom, calls=%fused_computation.clone | custom fusion | bytes 135168 | tf_op jit(solution)/shard_map/jit(_take)/gather | solution.py:104
  23.9 0.3 bitcast_multiply_fusion
  24.2 1.3 fusion.44
  25.9 0.2 fusion.29
  26.1 18.9 %psum.43 = f32[16,48]{1,0:T(8,128)S(1)} all-reduce(f32[16,48]{1,0:T(8,128)S(1)} %fusion.29), channel_id=1, replica_groups=mesh['parts'=2,'sub'=4,'row'=2,'col'=2] {'sub','row'}, use_global_device_ids=true, to_apply=%region_4.6 | all-reduce | flops 768 | bytes 6144 | tf_op jit(solution)/shard_map/psum | solution.py:83
  45.4 10.4 %while.20 = (s32[]{:T(128)}, f32[16,1024]{1,0:T(8,128)S(1)}, s32[]{:T(128)}, bf16[1024,2048]{1,0:T(8,128)(2,1)}, bf16[16,2048]{1,0:T(8,128)(2,1)S(1)}, /*index=5*/s32[]{:T(128)}, s32[]{:T(128)}, s32[]{:T(128)}, s32[]{:T(128)}) while((s32[]{:T(128)}, f32[16,1024]{1,0:T(8,128)S(1)}, s32[]{:T(128)}, bf16[1024,2048]{1,0:T(8,128)(2,1)}, ...), condition=%wide.region_3.5_spmd, body=%wide.region_2.4_spmd.sunk | while | flops 8388614 | bytes 599179 | solution.py:33
  45.4 1.3 fusion.71
  46.7 1.3 fusion.71
  48.0 1.3 fusion.71
  49.3 1.3 fusion.71
  50.6 1.3 fusion.71
  51.9 1.3 fusion.71
  53.2 1.3 fusion.71
  54.5 1.3 fusion.71
  55.9 4.6 %all-gather = bf16[32,1024]{1,0:T(8,128)(2,1)S(1)} all-gather(bf16[16,1024]{1,0:T(8,128)(2,1)S(1)} %fusion.6), channel_id=2, replica_groups=mesh['parts'=2,'sub'=4,'row'=2,'col'=2] {'row'}, dimensions={0}, use_global_device_ids=true | all-gather | bytes 98304 | tf_op jit(solution)/shard_map/all_gather | solution.py:89
  60.5 0.3 copy.47
  60.8 0.8 fusion.47
  61.6 3.8 %collective-permute-start.3 = (bf16[16,1024]{0,1:T(8,128)(2,1)S(1)}, bf16[16,1024]{0,1:T(8,128)(2,1)}, u32[]{:S(2)}, u32[]{:S(2)}) collective-permute-start(bf16[16,1024]{0,1:T(8,128)(2,1)S(1)} %get-tuple-element.151), channel_id=1, source_target_pairs={{0,12},{4,0},{8,4},{12,8},{1,13},{5,1},{9,5},{13,9},{2,14},{6,2},{... | collective-permute-start | bytes 98312 | tf_op jit(solution)/shard_map/ppermute | solution.py:13
  65.4 5.5 %collective-permute-done.3 = bf16[16,1024]{0,1:T(8,128)(2,1)} collective-permute-done((bf16[16,1024]{0,1:T(8,128)(2,1)S(1)}, bf16[16,1024]{0,1:T(8,128)(2,1)}, u32[]{:S(2)}, u32[]{:S(2)}) %collective-permute-start.3) | collective-permute-done | bytes 32800 | tf_op jit(solution)/shard_map/ppermute | solution.py:13
  70.9 1.0 convert_element_type.96
  71.9 4.0 %gather_fusion.3 = f32[1024,16]{1,0:T(8,128)} fusion(f32[16,1024]{0,1:T(8,128)S(1)} %convert_element_type.96, s32[1024]{0:T(1024)S(1)} %fusion.35), kind=kCustom, calls=%fused_computation.2.clone | custom fusion | bytes 135168 | tf_op jit(solution)/shard_map/jit(_take)/gather | solution.py:97
  76.0 4.0 %gather_fusion.2 = f32[1024,16]{1,0:T(8,128)} fusion(f32[16,1024]{0,1:T(8,128)S(1)} %convert_element_type.94, s32[1024]{0:T(1024)S(1)} %fusion.36), kind=kCustom, calls=%fused_computation.1.clone | custom fusion | bytes 135168 | tf_op jit(solution)/shard_map/jit(_take)/gather | solution.py:96
  80.0 2.8 %multiply_reduce_fusion.2 = (f32[16]{0:T(128)S(1)}, f32[16]{0:T(128)S(1)}, f32[16,1024]{0,1:T(8,128)}, f32[16,1024]{0,1:T(8,128)S(1)}) fusion(f32[16,2048]{0,1:T(8,128)} %get-tuple-element.145, f32[1024]{0:T(1024)S(1)} %get-tuple-element.156, f32[1024,16]{1,0:T(8,128)} %gather_fusion.2, pred[1024]{0:T(1024)(128)(4,1)S(1)} %compare_and_fusion, ...), kind=kLoop, calls=%fused_computation.42 | loop fusion | flops 180192 | bytes 534656 | tf_op jit(solution)/shard_map/reduce_sum | solution.py:17
  82.8 1.2 copy.48
  84.2 11.2 %all-reduce.1 = (f32[16]{0:T(128)S(1)}, f32[16]{0:T(128)S(1)}) all-reduce(f32[16]{0:T(128)S(1)} %get-tuple-element.112, f32[16]{0:T(128)S(1)} %get-tuple-element.111), channel_id=1, replica_groups=mesh['parts'=2,'sub'=4,'row'=2,'col'=2] {'sub'}, use_global_device_ids=true, to_apply=%region_1.3 | all-reduce | flops 32 | bytes 256 | tf_op jit(solution)/shard_map/psum | solution.py:21
  95.4 1.4 copy.51
  96.8 2.5 %fusion.41 = (bf16[16,2048]{0,1:T(8,128)(2,1)S(1)}, f32[16,2048]{0,1:T(8,128)S(1)}, f32[16,2048]{0,1:T(8,128)}) fusion(f32[2048]{0:T(1024)S(1)} %bitcast.101, f32[16,2048]{0,1:T(8,128)} %copy.51, f32[16,1024]{0,1:T(8,128)S(1)} %bitcast_multiply_fusion, f32[16,1024]{0,1:T(8,128)S(1)} %bitcast_multiply_fusion.1), kind=kLoop, calls=%fused_computation.88 | loop fusion | flops 131072 | bytes 598016 | tf_op jit(solution)/shard_map/convert_element_type | solution.py:75
  99.5 0.2 copy.52
  99.9 17.9 %psum.46 = f32[16,48]{1,0:T(8,128)S(1)} all-reduce(f32[16,48]{1,0:T(8,128)S(1)} %fusion.28), channel_id=1, replica_groups=mesh['parts'=2,'sub'=4,'row'=2,'col'=2] {'sub','row'}, use_global_device_ids=true, to_apply=%region_11.13 | all-reduce | flops 768 | bytes 6144 | tf_op jit(solution)/shard_map/psum | solution.py:83
  118.2 10.4 %while.21 = (s32[]{:T(128)}, f32[16,1024]{1,0:T(8,128)S(1)}, s32[]{:T(128)}, bf16[1024,2048]{1,0:T(8,128)(2,1)}, bf16[16,2048]{1,0:T(8,128)(2,1)S(1)}, /*index=5*/s32[]{:T(128)}, s32[]{:T(128)}, s32[]{:T(128)}, s32[]{:T(128)}) while((s32[]{:T(128)}, f32[16,1024]{1,0:T(8,128)S(1)}, s32[]{:T(128)}, bf16[1024,2048]{1,0:T(8,128)(2,1)}, ...), condition=%wide.region_10.12_spmd, body=%wide.region_9.11_spmd.sunk | while | flops 8388614 | bytes 599179 | solution.py:33
  118.2 1.3 fusion.74
  119.5 1.3 fusion.74
  120.8 1.3 fusion.74
  122.1 1.3 fusion.74
  123.4 1.3 fusion.74
  124.6 1.3 fusion.74
  125.9 1.3 fusion.74
  127.2 1.3 fusion.74
  128.7 4.6 %all-gather.1 = bf16[32,1024]{1,0:T(8,128)(2,1)S(1)} all-gather(bf16[16,1024]{1,0:T(8,128)(2,1)S(1)} %fusion.7), channel_id=3, replica_groups=mesh['parts'=2,'sub'=4,'row'=2,'col'=2] {'row'}, dimensions={0}, use_global_device_ids=true | all-gather | bytes 98304 | tf_op jit(solution)/shard_map/all_gather | solution.py:89
  133.3 0.3 copy.53
  133.6 0.8 fusion.46
  134.4 2.0 %collective-permute-start.4 = (bf16[16,1024]{0,1:T(8,128)(2,1)}, bf16[16,1024]{0,1:T(8,128)(2,1)}, u32[]{:S(2)}, u32[]{:S(2)}) collective-permute-start(bf16[16,1024]{0,1:T(8,128)(2,1)} %get-tuple-element.148), channel_id=1, source_target_pairs={{0,4},{4,8},{8,12},{12,0},{1,5},{5,9},{9,13},{13,1},{2,6},{6,10},{... | collective-permute-start | bytes 98312 | tf_op jit(solution)/shard_map/ppermute | solution.py:13
  136.4 7.2 %collective-permute-done.5 = bf16[16,1024]{0,1:T(8,128)(2,1)S(1)} collective-permute-done((bf16[16,1024]{0,1:T(8,128)(2,1)S(1)}, bf16[16,1024]{0,1:T(8,128)(2,1)S(1)}, u32[]{:S(2)}, u32[]{:S(2)}) %collective-permute-start.5) | collective-permute-done | bytes 32800 | tf_op jit(solution)/shard_map/ppermute | solution.py:13
  143.6 0.8 convert_element_type.106
  144.4 5.1 %gather_fusion.5 = f32[1024,16]{1,0:T(8,128)} fusion(f32[16,1024]{0,1:T(8,128)} %convert_element_type.106, s32[1024]{0:T(1024)S(1)} %fusion.35), kind=kCustom, calls=%fused_computation.4.clone | custom fusion | bytes 135168 | tf_op jit(solution)/shard_map/jit(_take)/gather | solution.py:97
  149.5 1.8 %convert_element_type.104 = f32[16,1024]{0,1:T(8,128)} convert(bf16[16,1024]{0,1:T(8,128)(2,1)} %collective-permute-done.4) | non-fusion elementwise | flops 16384 | bytes 98304 | tf_op jit(solution)/shard_map/convert_element_type | solution.py:94
  151.3 5.1 %gather_fusion.4 = f32[1024,16]{1,0:T(8,128)} fusion(f32[16,1024]{0,1:T(8,128)} %convert_element_type.104, s32[1024]{0:T(1024)S(1)} %fusion.36), kind=kCustom, calls=%fused_computation.3.clone | custom fusion | bytes 135168 | tf_op jit(solution)/shard_map/jit(_take)/gather | solution.py:96
  156.3 2.9 %multiply_reduce_fusion = (f32[16]{0:T(128)S(1)}, f32[16]{0:T(128)S(1)}, f32[16,1024]{0,1:T(8,128)}, f32[16,1024]{0,1:T(8,128)}) fusion(f32[16,2048]{0,1:T(8,128)S(1)} %get-tuple-element.141, f32[16,2048]{0,1:T(8,128)} %get-tuple-element.142, f32[1024]{0:T(1024)S(1)} %get-tuple-element.156, f32[1024,16]{1,0:T(8,128)} %gather_fusion.4, ...), kind=kLoop, calls=%fused_computation.40 | loop fusion | flops 163808 | bytes 534656 | tf_op jit(solution)/shard_map/reduce_sum | solution.py:17
  159.2 8.3 %all-reduce = (f32[16]{0:T(128)S(1)}, f32[16]{0:T(128)S(1)}) all-reduce(f32[16]{0:T(128)S(1)} %get-tuple-element.110, f32[16]{0:T(128)S(1)} %get-tuple-element.109), channel_id=1, replica_groups=mesh['parts'=2,'sub'=4,'row'=2,'col'=2] {'sub'}, use_global_device_ids=true, to_apply=%region_8.10 | all-reduce | flops 32 | bytes 256 | tf_op jit(solution)/shard_map/psum | solution.py:21
  167.9 2.2 %fusion.13 = (f32[1,16,1024]{1,2,0:T(8,128)}, f32[1,16,1024]{1,2,0:T(8,128)S(1)}) fusion(f32[16,1024]{0,1:T(8,128)S(1)} %copy.59, f32[16,1024]{0,1:T(8,128)} %get-tuple-element.146, f32[16,1024]{0,1:T(8,128)} %get-tuple-element.139, f32[16,2048]{0,1:T(8,128)} %get-tuple-element.142, f32[16]{0:T(128)S(1)} %get-tuple-element.137, ...), kind=kLoop, calls=%fused_computation.27 | loop fusion | flops 147456 | bytes 524480 | tf_op jit(solution)/shard_map/broadcast_in_dim | solution.py:127
  170.1 1.8 %copy.57 = f32[1,16,1024]{2,1,0:T(8,128)} copy(f32[1,16,1024]{1,2,0:T(8,128)} %get-tuple-element.152) | data formatting | bytes 131072
  171.9 0.8 copy.56
  (48 shorter events, 2.7 us)
Async XLA Ops:
  0.6 25.1 %copy-start = (bf16[1,24,1024]{2,1,0:T(8,128)(2,1)S(1)}, bf16[1,24,1024]{2,1,0:T(8,128)(2,1)}, u32[]{:S(2)}) copy-start(bf16[1,24,1024]{2,1,0:T(8,128)(2,1)} %param.18) | copy-start | bytes 147460
  0.6 20.3 %copy-start.5 = (f32[1,1024]{1,0:T(1,128)S(1)}, f32[1,1024]{1,0:T(1,128)}, u32[]{:S(2)}) copy-start(f32[1,1024]{1,0:T(1,128)} %param.16) | copy-start | bytes 12292
  0.7 20.3 %copy-start.2 = (s32[1,1024]{1,0:T(1,128)S(1)}, s32[1,1024]{1,0:T(1,128)}, u32[]{:S(2)}) copy-start(s32[1,1024]{1,0:T(1,128)} %param.23) | copy-start | bytes 12292
  1.4 15.0 %collective-permute-start = (bf16[1,1024]{1,0:T(2,128)(2,1)S(1)}, bf16[1,1024]{1,0:T(2,128)(2,1)S(1)}, u32[]{:S(2)}, u32[]{:S(2)}) collective-permute-start(bf16[1,1024]{1,0:T(2,128)(2,1)S(1)} %convert_element_type.83), channel_id=1, source_target_pairs={{0,12},{4,0},{8,4},{12,8},{1,13},{5,1},{9,5},{13,9},{2,14},{6,2},{... | collective-permute-start | bytes 6152 | tf_op jit(solution)/shard_map/ppermute | solution.py:13
  7.6 13.4 %collective-permute-start.1 = (bf16[16,1024]{0,1:T(8,128)(2,1)S(1)}, bf16[16,1024]{0,1:T(8,128)(2,1)S(1)}, u32[]{:S(2)}, u32[]{:S(2)}) collective-permute-start(bf16[16,1024]{0,1:T(8,128)(2,1)S(1)} %bitcast_convert_fusion), channel_id=1, source_target_pairs={{0,12},{4,0},{8,4},{12,8},{1,13},{5,1},{9,5},{13,9},{2,14},{6,2},{... | collective-permute-start | bytes 98312 | tf_op jit(solution)/shard_map/ppermute | solution.py:13
  16.4 28.6 %copy-start.3 = (f32[48,48]{1,0:T(8,128)S(1)}, f32[48,48]{1,0:T(8,128)}, u32[]{:S(2)}) copy-start(f32[48,48]{1,0:T(8,128)} %param.19) | copy-start | bytes 27652
  24.2 41.2 %copy-start.4 = (s32[1,1024]{1,0:T(1,128)S(1)}, s32[1,1024]{1,0:T(1,128)}, u32[]{:S(2)}) copy-start(s32[1,1024]{1,0:T(1,128)} %param.22) | copy-start | bytes 12292
  61.6 14.3 %collective-permute-start.2 = (bf16[16,1024]{0,1:T(8,128)(2,1)}, bf16[16,1024]{0,1:T(8,128)(2,1)S(1)}, u32[]{:S(2)}, u32[]{:S(2)}) collective-permute-start(bf16[16,1024]{0,1:T(8,128)(2,1)} %get-tuple-element.150), channel_id=1, source_target_pairs={{0,4},{4,8},{8,12},{12,0},{1,5},{5,9},{9,13},{13,1},{2,6},{6,10},{... | collective-permute-start | bytes 98312 | tf_op jit(solution)/shard_map/ppermute | solution.py:13
  61.6 9.3 %collective-permute-start.3 = (bf16[16,1024]{0,1:T(8,128)(2,1)S(1)}, bf16[16,1024]{0,1:T(8,128)(2,1)}, u32[]{:S(2)}, u32[]{:S(2)}) collective-permute-start(bf16[16,1024]{0,1:T(8,128)(2,1)S(1)} %get-tuple-element.151), channel_id=1, source_target_pairs={{0,12},{4,0},{8,4},{12,8},{1,13},{5,1},{9,5},{13,9},{2,14},{6,2},{... | collective-permute-start | bytes 98312 | tf_op jit(solution)/shard_map/ppermute | solution.py:13
  134.4 33.5 %copy-start.1 = (f32[16,2048]{0,1:T(8,128)S(1)}, f32[16,2048]{0,1:T(8,128)}, u32[]{:S(2)}) copy-start(f32[16,2048]{0,1:T(8,128)} %get-tuple-element.145) | copy-start | bytes 393220
  134.4 9.2 %collective-permute-start.5 = (bf16[16,1024]{0,1:T(8,128)(2,1)S(1)}, bf16[16,1024]{0,1:T(8,128)(2,1)S(1)}, u32[]{:S(2)}, u32[]{:S(2)}) collective-permute-start(bf16[16,1024]{0,1:T(8,128)(2,1)S(1)} %get-tuple-element.147), channel_id=1, source_target_pairs={{0,12},{4,0},{8,4},{12,8},{1,13},{5,1},{9,5},{13,9},{2,14},{6,2},{... | collective-permute-start | bytes 98312 | tf_op jit(solution)/shard_map/ppermute | solution.py:13
  134.4 15.1 %collective-permute-start.4 = (bf16[16,1024]{0,1:T(8,128)(2,1)}, bf16[16,1024]{0,1:T(8,128)(2,1)}, u32[]{:S(2)}, u32[]{:S(2)}) collective-permute-start(bf16[16,1024]{0,1:T(8,128)(2,1)} %get-tuple-element.148), channel_id=1, source_target_pairs={{0,4},{4,8},{8,12},{12,0},{1,5},{5,9},{9,13},{13,1},{2,6},{6,10},{... | collective-permute-start | bytes 98312 | tf_op jit(solution)/shard_map/ppermute | solution.py:13
